TPU v7x, 512 devices: a whole 4x8x8 slice. The times are simulated.
512 devices in a mesh: row: 16 (over y, z_lo), col: 32 (over z_hi, x, core).
Axes of the slice: x: 4, y: 8, z: 8 (z_hi: 4, z_lo: 2; z = z_hi * 2 + z_lo), core: 2. Of those that a mesh axis runs over, the one named last changes fastest.
Arguments:
- tiles: bfloat16 [16, 32, 32, 256, 256], P('row', 'col'), may hold values from -6 to 6
- tile_ids: int32 [16, 32, 2, 32], P('row', 'col'), may hold values from 0 to 7, as said below
- tile_count: int32 [16, 32], P('row', 'col'), may hold values from 8 to 32
- query_degree: int32 [32768], P('row'), may hold values from 1 to 32
- product_degree: int32 [65536], P('col'), may hold values from 1 to 32
- panel: float32 [64, 65536], P(None, ('col', 'row')), may hold values from -6 to 6
Outputs:
- basis: float32 [64, 65536], P(None, ('col', 'row'))
Inputs may be any that keep to these rules, and one draw needn't show every extreme that they name: `tile_ids`: on each device the 32 (tile row, tile column) pairs are distinct; tile row is below 8 and tile column below 8.
All inputs are finite; a program needn't handle non-finite values.
Results may differ from a plain program's by a relative error of at most 0.0042.
Values may be sent and summed in bfloat16 or wider, within the bound.
A program may use at most 64 MiB of HBM per device.

v0:
```python
import math
import jax
import jax.numpy as jnp
from jax import lax
from jax.sharding import PartitionSpec as P

ITERS = 2
HIGH = lax.Precision.HIGHEST


def orthonormal(lifted, gram):
    lower = jnp.linalg.cholesky(gram)
    return lax.linalg.triangular_solve(lower, lifted, left_side=True, lower=True)


def shards(tiles, tile_ids, tile_count, query_degree, product_degree, panel):
    tile_set = tiles[0, 0]
    slot_ids = tile_ids[0, 0]
    live_count = tile_count[0, 0]
    slots = tile_set.shape[0]
    side = tile_set.shape[1]
    width = panel.shape[0]
    query_tiles = query_degree.shape[0] // side
    product_tiles = product_degree.shape[0] // side
    live_slot = (jnp.arange(slots, dtype=jnp.int32) < live_count).astype(jnp.float32)
    row_hot = (slot_ids[0][:, None] == jnp.arange(query_tiles, dtype=jnp.int32)[None, :]).astype(
        jnp.float32
    ) * live_slot[:, None]
    col_hot = (slot_ids[1][:, None] == jnp.arange(product_tiles, dtype=jnp.int32)[None, :]).astype(
        jnp.float32
    ) * live_slot[:, None]
    qscale = 1.0 / jnp.sqrt(query_degree.astype(jnp.float32))
    pscale = 1.0 / jnp.sqrt(product_degree.astype(jnp.float32))
    row_at = lax.axis_index("row")
    col_at = lax.axis_index("col")
    share = panel.shape[1]
    my_pscale = lax.dynamic_slice_in_dim(pscale, row_at * share, share)
    root_count = math.sqrt(product_degree.shape[0] * lax.axis_size("col"))
    current = panel
    for iteration in range(ITERS):
        scaled = (current * my_pscale[None, :]).astype(jnp.bfloat16)
        scaled_block = lax.all_gather(scaled, "row", axis=1, tiled=True)
        picked = jnp.take(scaled_block.reshape(width, product_tiles, side), slot_ids[1], axis=1)
        products = jnp.einsum("rkj,kij->kri", picked, tile_set, preferred_element_type=jnp.float32)
        partial_sum = jnp.einsum("kq,kri->rqi", row_hot, products, precision=HIGH).reshape(
            width, query_tiles * side
        )
        query_share = lax.psum_scatter(partial_sum, "col", scatter_dimension=1, tiled=True)
        columns = query_share.shape[1]
        my_qscale = lax.dynamic_slice_in_dim(qscale, col_at * columns, columns)
        rounded = (query_share * my_qscale[None, :]).astype(jnp.bfloat16)
        query_block = lax.all_gather(rounded, "col", axis=1, tiled=True)
        backward_picked = jnp.take(
            query_block.reshape(width, query_tiles, side), slot_ids[0], axis=1
        )
        backward_products = jnp.einsum(
            "rki,kij->krj", backward_picked, tile_set, preferred_element_type=jnp.float32
        )
        lifted = (
            lax.psum_scatter(
                jnp.einsum("kp,krj->rpj", col_hot, backward_products, precision=HIGH).reshape(
                    width, product_tiles * side
                ),
                "row",
                scatter_dimension=1,
                tiled=True,
            )
            * my_pscale[None, :]
        )
        gram = lax.psum(jnp.einsum("ri,si->rs", lifted, lifted, precision=HIGH), ("row", "col"))
        current = orthonormal(lifted, gram)
    return current * root_count


def solution(mesh):
    in_specs = (
        P("row", "col", None, None, None),
        P("row", "col", None, None),
        P("row", "col"),
        P("row"),
        P("col"),
        P(None, ("col", "row")),
    )
    out_specs = P(None, ("col", "row"))
    return jax.shard_map(shards, mesh=mesh, in_specs=in_specs, out_specs=out_specs, check_vma=False)
```

profile of v0, /device:TPU:24, one launch (start us, length us, event | category | flops | bytes accessed | tf_op | source)
XLA Modules:
  0.0 757.7 jit_solution(1532699937566994767)
XLA Ops:
  10.3 32.3 %all_gather.12 = bf16[64,2048]{1,0:T(8,128)(2,1)S(1)} all-gather(bf16[64,128]{1,0:T(8,128)(2,1)S(1)} %multiply_convert_fusion.2), channel_id=1, replica_groups=mesh['row'=16,'col'=32] {'row'}, dimensions={1}, use_global_device_ids=true | all-gather | bytes 278528 | tf_op jit(solution)/shard_map/all_gather | solution.py:42
  43.2 3.6 fusion.6
  46.8 2.4 fusion.16
  49.1 1.4 copy.55
  51.3 101.7 %reduce-scatter.13.cloned.1.call-done = f32[64,64]{1,0:T(8,128)} async-done(((f32[2048,64]{1,0:T(8,128)}), f32[64,64]{1,0:T(8,128)}) %reduce-scatter.13.cloned.1.call-update) | async-done | bytes 16400
  153.1 0.8 copy.52
  154.0 43.8 %all_gather.13 = bf16[64,2048]{0,1:T(8,128)(2,1)S(1)} all-gather(bf16[64,64]{0,1:T(8,128)(2,1)S(1)} %copy.31), channel_id=1, replica_groups=mesh['row'=16,'col'=32] {'col'}, dimensions={1}, use_global_device_ids=true | all-gather | bytes 270336 | tf_op jit(solution)/shard_map/all_gather | solution.py:52
  198.6 3.1 fusion.4
  201.7 2.4 fusion.12
  204.1 1.0 copy.59
  205.1 67.3 %reduce-scatter.9.cloned.1.call-done = f32[64,128]{1,0:T(8,128)} async-done(((f32[64,2048]{1,0:T(8,128)}), f32[64,128]{1,0:T(8,128)}) %reduce-scatter.9.cloned.1.call-update) | async-done | bytes 32784 | tf_op jit(solution)/shard_map/reduce_scatter | solution.py:60
  272.4 1.0 fusion.51
  273.4 98.9 %psum.14 = f32[64,64]{0,1:T(8,128)S(1)} all-reduce(f32[64,64]{0,1:T(8,128)S(1)} %fusion.51), channel_id=1, replica_groups=mesh['row'=16,'col'=32] {'row','col'}, use_global_device_ids=true, to_apply=%region_2.4 | all-reduce | flops 4096 | bytes 32768 | tf_op jit(solution)/shard_map/psum | solution.py:70
  372.5 5.8 cholesky.44
  379.6 4.9 custom-call.6
  384.5 1.0 fusion.22
  385.6 29.2 %all_gather.14 = bf16[64,2048]{1,0:T(8,128)(2,1)S(1)} all-gather(bf16[64,128]{1,0:T(8,128)(2,1)S(1)} %fusion.22), channel_id=1, replica_groups=mesh['row'=16,'col'=32] {'row'}, dimensions={1}, use_global_device_ids=true | all-gather | bytes 278528 | tf_op jit(solution)/shard_map/all_gather | solution.py:42
  415.4 3.6 fusion.2
  419.0 2.4 fusion.19
  421.4 1.4 copy.56
  422.8 95.3 %reduce-scatter.15.cloned.1.call-done = f32[64,64]{1,0:T(8,128)} async-done(((f32[2048,64]{1,0:T(8,128)}), f32[64,64]{1,0:T(8,128)}) %reduce-scatter.15.cloned.1.call-update) | async-done | bytes 16400
  518.1 0.8 copy.54
  519.0 43.8 %all_gather.15 = bf16[64,2048]{0,1:T(8,128)(2,1)S(1)} all-gather(bf16[64,64]{0,1:T(8,128)(2,1)S(1)} %copy.39), channel_id=1, replica_groups=mesh['row'=16,'col'=32] {'col'}, dimensions={1}, use_global_device_ids=true | all-gather | bytes 270336 | tf_op jit(solution)/shard_map/all_gather | solution.py:52
  563.6 3.1 fusion
  566.7 2.4 fusion.8
  569.1 1.0 copy.60
  570.1 67.3 %reduce-scatter.11.cloned.1.call-done = f32[64,128]{1,0:T(8,128)} async-done(((f32[64,2048]{1,0:T(8,128)}), f32[64,128]{1,0:T(8,128)}) %reduce-scatter.11.cloned.1.call-update) | async-done | bytes 32784 | tf_op jit(solution)/shard_map/reduce_scatter | solution.py:60
  637.4 1.0 fusion.48
  638.4 99.0 %psum.15 = f32[64,64]{0,1:T(8,128)S(1)} all-reduce(f32[64,64]{0,1:T(8,128)S(1)} %fusion.48), channel_id=1, replica_groups=mesh['row'=16,'col'=32] {'row','col'}, use_global_device_ids=true, to_apply=%region_7.11 | all-reduce | flops 4096 | bytes 32768 | tf_op jit(solution)/shard_map/psum | solution.py:70
  737.5 5.8 cholesky.55
  744.7 4.9 custom-call.7
  749.6 1.6 convolution_multiply_fusion
  (38 shorter events, 9.9 us)
Async XLA Ops:
  6.5 146.5 %reduce-scatter.13.cloned.1.call-start = ((), (), s32[]{:S(2)}) async-start(), calls=%async_computation.6 | async-start | bytes 1081344
  50.5 221.9 %reduce-scatter.9.cloned.1.call-start = ((), (), s32[]{:S(2)}) async-start(), calls=%async_computation.4 | async-start | bytes 557056 | tf_op jit(solution)/shard_map/reduce_scatter | solution.py:60
  205.0 313.1 %reduce-scatter.15.cloned.1.call-start = ((), (), s32[]{:S(2)}) async-start(), calls=%async_computation.7 | async-start | bytes 1081344
  422.8 214.6 %reduce-scatter.11.cloned.1.call-start = ((), (), s32[]{:S(2)}) async-start(), calls=%async_computation.5 | async-start | bytes 557056 | tf_op jit(solution)/shard_map/reduce_scatter | solution.py:60
Sparse Core Ops, SparseCore 0:
  50.6 102.3 reduce-scatter.12
  205.2 67.2 reduce-scatter.8
  422.9 95.1 reduce-scatter.14
  570.2 67.1 reduce-scatter.10
where the time goes:
time: 759 us; the launch traced here: 758 us
  blocking collectives  347 us (46%)
  waiting for transfers between devices  332 us (44%)
  matrix products  27.4 us (4%)
  other arithmetic  27.3 us (4%)
  between operations  14 us (2%)
  local copies, waits for them, and re-layouts  10.3 us (1%)
    psum x2, blocking collectives, shards(): lax.psum(jnp.einsum('ri,si->rs', lifted, lifted, precision=HIGH), ('row',...  198 us
    unnamed x6, waiting for transfers between devices  197 us
    reduce_scatter x2, waiting for transfers between devices, shards(): lax.psum_scatter(jnp.einsum('kp,krj->rpj', col_hot, backward_products, pr...  135 us
    all_gather x2, blocking collectives, shards(): query_block = lax.all_gather(rounded, 'col', axis=1, tiled=True)  87.6 us
    all_gather x2, blocking collectives, shards(): scaled_block = lax.all_gather(scaled, 'row', axis=1, tiled=True)  61.5 us
  transfers between devices with their start and end apart: 4, of which 4 were waited for; matrix products, arithmetic and copies ran while one was open for 0% of the time, Pallas kernels for 0%

commit v1 on v0

--- a/solution.py
+++ b/solution.py
@@ -67,7 +67,10 @@
             )
             * my_pscale[None, :]
         )
-        gram = lax.psum(jnp.einsum("ri,si->rs", lifted, lifted, precision=HIGH), ("row", "col"))
+        gram = jnp.sum(
+            lax.all_gather(jnp.einsum("ri,si->rs", lifted, lifted, precision=HIGH), ("row", "col")),
+            axis=0,
+        )
         current = orthonormal(lifted, gram)
     return current * root_count
 

time: 759 us -> 2240 us (2.95)
  the two profiles are of different devices: /device:TPU:24 before, /device:TPU:2 now
where the time goes in v1:
time: 2240 us
  waiting for transfers between devices  2000 us (89%)
  blocking collectives  151 us (7%)
  other arithmetic  41.1 us (2%)
  matrix products  27.1 us (1%)
    all_gather x2, waiting for transfers between devices, shards(): lax.all_gather(jnp.einsum('ri,si->rs', lifted, lifted, precision=HIGH), (...  1660 us
    unnamed x8, waiting for transfers between devices  194 us
    reduce_scatter x2, waiting for transfers between devices, shards(): lax.psum_scatter(jnp.einsum('kp,krj->rpj', col_hot, backward_products, pr...  145 us
    all_gather x2, blocking collectives, shards(): query_block = lax.all_gather(rounded, 'col', axis=1, tiled=True)  82.7 us
    all_gather x2, blocking collectives, shards(): scaled_block = lax.all_gather(scaled, 'row', axis=1, tiled=True)  68.8 us
  transfers between devices with their start and end apart: 6, of which 6 were waited for; matrix products, arithmetic and copies ran while one was open for 0% of the time, Pallas kernels for 0%

profile of v1, /device:TPU:2, one launch (start us, length us, event | category | flops | bytes accessed | tf_op | source)
XLA Modules:
  0.0 2244.2 jit_solution(18358841044332917380)
XLA Ops:
  10.3 36.3 %all_gather.24 = bf16[64,2048]{1,0:T(8,128)(2,1)S(1)} all-gather(bf16[64,128]{1,0:T(8,128)(2,1)S(1)} %multiply_convert_fusion.2), channel_id=1, replica_groups=mesh['row'=16,'col'=32] {'row'}, dimensions={1}, use_global_device_ids=true | all-gather | bytes 278528 | tf_op jit(solution)/shard_map/all_gather | solution.py:42
  47.3 3.6 fusion.6
  50.8 2.4 fusion.16
  53.2 1.4 copy.45
  55.4 97.3 %reduce-scatter.13.cloned.1.call-done = f32[64,64]{1,0:T(8,128)} async-done(((f32[2048,64]{1,0:T(8,128)}), f32[64,64]{1,0:T(8,128)}) %reduce-scatter.13.cloned.1.call-update) | async-done | bytes 16400
  152.7 0.8 copy.42
  153.7 41.4 %all_gather.25 = bf16[64,2048]{0,1:T(8,128)(2,1)S(1)} all-gather(bf16[64,64]{0,1:T(8,128)(2,1)S(1)} %copy.25), channel_id=1, replica_groups=mesh['row'=16,'col'=32] {'col'}, dimensions={1}, use_global_device_ids=true | all-gather | bytes 270336 | tf_op jit(solution)/shard_map/all_gather | solution.py:52
  195.9 3.1 fusion.4
  198.9 2.4 fusion.12
  201.3 1.0 copy.49
  202.3 72.4 %reduce-scatter.9.cloned.1.call-done = f32[64,128]{1,0:T(8,128)} async-done(((f32[64,2048]{1,0:T(8,128)}), f32[64,128]{1,0:T(8,128)}) %reduce-scatter.9.cloned.1.call-update) | async-done | bytes 32784 | tf_op jit(solution)/shard_map/reduce_scatter | solution.py:60
  274.7 1.6 fusion.51
  276.4 830.5 %all-gather.5.cloned.1.call-done = f32[32768,64]{1,0:T(8,128)} async-done(((f32[64,64]{1,0:T(8,128)}), f32[32768,64]{1,0:T(8,128)}) %all-gather.5.cloned.1.call-update) | async-done | bytes 8388624 | tf_op jit(solution)/shard_map/all_gather | solution.py:71
  1106.9 6.9 reduce_sum.18
  1114.0 5.8 cholesky.44
  1121.1 4.9 custom-call.6
  1126.3 32.5 %all_gather.28 = bf16[64,2048]{1,0:T(8,128)(2,1)S(1)} all-gather(bf16[64,128]{1,0:T(8,128)(2,1)S(1)} %fusion.22), channel_id=1, replica_groups=mesh['row'=16,'col'=32] {'row'}, dimensions={1}, use_global_device_ids=true | all-gather | bytes 278528 | tf_op jit(solution)/shard_map/all_gather | solution.py:42
  1159.4 3.6 fusion.2
  1163.0 2.4 fusion.19
  1165.3 1.4 copy.46
  1166.8 96.5 %reduce-scatter.15.cloned.1.call-done = f32[64,64]{1,0:T(8,128)} async-done(((f32[2048,64]{1,0:T(8,128)}), f32[64,64]{1,0:T(8,128)}) %reduce-scatter.15.cloned.1.call-update) | async-done | bytes 16400
  1264.2 41.3 %all_gather.29 = bf16[64,2048]{0,1:T(8,128)(2,1)S(1)} all-gather(bf16[64,64]{0,1:T(8,128)(2,1)S(1)} %copy.32), channel_id=1, replica_groups=mesh['row'=16,'col'=32] {'col'}, dimensions={1}, use_global_device_ids=true | all-gather | bytes 270336 | tf_op jit(solution)/shard_map/all_gather | solution.py:52
  1306.4 3.1 fusion
  1309.5 2.4 fusion.8
  1311.8 1.0 copy.50
  1312.9 72.4 %reduce-scatter.11.cloned.1.call-done = f32[64,128]{1,0:T(8,128)} async-done(((f32[64,2048]{1,0:T(8,128)}), f32[64,128]{1,0:T(8,128)}) %reduce-scatter.11.cloned.1.call-update) | async-done | bytes 32784 | tf_op jit(solution)/shard_map/reduce_scatter | solution.py:60
  1385.3 1.6 fusion.48
  1386.9 830.4 %all-gather.7.cloned.1.call-done = f32[32768,64]{1,0:T(8,128)} async-done(((f32[64,64]{1,0:T(8,128)}), f32[32768,64]{1,0:T(8,128)}) %all-gather.7.cloned.1.call-update) | async-done | bytes 8388624 | tf_op jit(solution)/shard_map/all_gather | solution.py:71
  2217.3 6.9 reduce_sum.19
  2224.4 5.8 cholesky.55
  2231.6 4.9 custom-call.7
  2236.5 0.9 convolution_multiply_fusion
  (48 shorter events, 11.1 us)
Async XLA Ops:
  6.5 146.2 %reduce-scatter.13.cloned.1.call-start = ((), (), s32[]{:S(2)}) async-start(), calls=%async_computation.8 | async-start | bytes 1081344
  54.6 220.1 %reduce-scatter.9.cloned.1.call-start = ((), (), s32[]{:S(2)}) async-start(), calls=%async_computation.4 | async-start | bytes 557056 | tf_op jit(solution)/shard_map/reduce_scatter | solution.py:60
  202.3 904.6 %all-gather.5.cloned.1.call-start = ((), (), s32[]{:S(2)}) async-start(), calls=%async_computation.6 | async-start | bytes 16809984 | tf_op jit(solution)/shard_map/all_gather | solution.py:71
  276.4 986.9 %reduce-scatter.15.cloned.1.call-start = ((), (), s32[]{:S(2)}) async-start(), calls=%async_computation.9 | async-start | bytes 1081344
  1106.9 19.1 copy-start.1
  1166.7 218.5 %reduce-scatter.11.cloned.1.call-start = ((), (), s32[]{:S(2)}) async-start(), calls=%async_computation.5 | async-start | bytes 557056 | tf_op jit(solution)/shard_map/reduce_scatter | solution.py:60
  1312.8 904.5 %all-gather.7.cloned.1.call-start = ((), (), s32[]{:S(2)}) async-start(), calls=%async_computation.7 | async-start | bytes 16809984 | tf_op jit(solution)/shard_map/all_gather | solution.py:71
  2217.3 19.1 copy-start
Sparse Core Ops, SparseCore 0:
  54.7 97.9 reduce-scatter.12
  202.4 72.2 reduce-scatter.8
  276.9 829.9 all-gather.4
  1166.9 96.3 reduce-scatter.14
  1312.9 72.2 reduce-scatter.10
  1387.3 829.9 all-gather.6
